TPU v7x, 32 devices: a whole 2x2x4 slice. The times are simulated.
32 devices in a mesh: leaf: 2 (over core), row: 4 (over z), col: 4 (over y, x).
Axes of the slice: x: 2, y: 2, z: 4, core: 2. Of those that a mesh axis runs over, the one named last changes fastest.
Arguments:
- hidden_in: bfloat16 [10240, 2048], P(('leaf', 'row', 'col')), may hold values from -6 to 6
- per_layer_in: bfloat16 [10240, 256], P(('leaf', 'row', 'col')), may hold values from -6 to 6
- cotangent: bfloat16 [10240, 2048], P(('leaf', 'row', 'col')), may hold values from -6 to 6
- norm_in: float32 [2048], replicated, may hold values from 0.25 to 1.75
- w_query: bfloat16 [2048, 2048], P(None, 'row'), may hold values from -0.125 to 0.125
- w_key: bfloat16 [2048, 512], replicated, may hold values from -0.125 to 0.125
- w_value: bfloat16 [2048, 512], replicated, may hold values from -0.125 to 0.125
- query_norm: float32 [256], replicated, may hold values from 0.25 to 1.75
- key_norm: float32 [256], replicated, may hold values from 0.25 to 1.75
- w_out: bfloat16 [2048, 2048], P('row'), may hold values from -0.125 to 0.125
- post_attn_norm: float32 [2048], replicated, may hold values from 0.25 to 1.75
- laurel_left: bfloat16 [2048, 64], replicated, may hold values from -0.125 to 0.125
- laurel_right: bfloat16 [64, 2048], replicated, may hold values from -0.75 to 0.75
- laurel_norm: float32 [2048], replicated, may hold values from 0.25 to 1.75
- pre_ffn_norm: float32 [2048], replicated, may hold values from 0.25 to 1.75
- w_gate: bfloat16 [2048, 8192], P(None, 'row'), may hold values from -0.125 to 0.125
- w_up: bfloat16 [2048, 8192], P(None, 'row'), may hold values from -0.125 to 0.125
- w_down: bfloat16 [8192, 2048], P('row'), may hold values from -0.0625 to 0.0625
- post_ffn_norm: float32 [2048], replicated, may hold values from 0.25 to 1.75
- per_layer_gate: bfloat16 [2048, 256], replicated, may hold values from -0.125 to 0.125
- per_layer_proj: bfloat16 [256, 2048], replicated, may hold values from -0.375 to 0.375
- per_layer_norm: float32 [2048], replicated, may hold values from 0.25 to 1.75
- parents: int32 [26], replicated, may hold values from 0 to 25, as said below
- segment: int32 [10240], replicated, may hold values from 0 to 25, as said below
- position: int32 [10240], replicated, may hold values from 0 to 2559, as said below
Outputs:
- output: float32 [10240, 2048], P(('leaf', 'row', 'col'))
- input_grad: float32 [10240, 2048], P(('leaf', 'row', 'col'))
- per_layer_in_grad: float32 [10240, 256], P(('leaf', 'row', 'col'))
- norm_in_grad: float32 [2048], replicated
- w_query_grad: float32 [2048, 2048], P(('leaf', 'col'), 'row')
- w_key_grad: float32 [2048, 512], P(None, 'row')
- w_value_grad: float32 [2048, 512], P(None, 'row')
- query_norm_grad: float32 [256], replicated
- key_norm_grad: float32 [256], replicated
- w_out_grad: float32 [2048, 2048], P('row', ('leaf', 'col'))
- post_attn_norm_grad: float32 [2048], replicated
- laurel_left_grad: float32 [2048, 64], replicated
- laurel_right_grad: float32 [64, 2048], replicated
- laurel_norm_grad: float32 [2048], replicated
- pre_ffn_norm_grad: float32 [2048], replicated
- w_gate_grad: float32 [2048, 8192], P(('leaf', 'col'), 'row')
- w_up_grad: float32 [2048, 8192], P(('leaf', 'col'), 'row')
- w_down_grad: float32 [8192, 2048], P('row', ('leaf', 'col'))
- post_ffn_norm_grad: float32 [2048], replicated
- per_layer_gate_grad: float32 [2048, 256], replicated
- per_layer_proj_grad: float32 [256, 2048], replicated
- per_layer_norm_grad: float32 [2048], replicated
Inputs may be any that keep to these rules, and one draw needn't show every extreme that they name: parents[s] is the segment that segment s continues: every tree has one trunk of 2048 tokens that names itself, four branches of 256 tokens that name the trunk, and eight leaves of 256 tokens, two on each branch, that name their branch; segment numbers are drawn at random. Reading the tokens of one leaf index in the order of col index, then row index, then a device's rows, each tree fills 5120 consecutive tokens, and the tokens of each segment lie together, segments in an order drawn for each tree. `position`: A token's place on its path: a trunk's tokens take 0 to 2047, a branch's start at 2048, a leaf's at 2304, rising by one within a segment.
All inputs are finite; a program needn't handle non-finite values.
Results may differ from a plain program's by a relative error of at most 0.022.
Values may be sent and summed in bfloat16 or wider, within the bound.
A program may use at most 384 MiB of HBM per device.

v0:
```python
import math

import jax
import jax.numpy as jnp
from jax import lax
from jax.sharding import PartitionSpec as P

H = 8
KV = 2
HD = 256
TRUNK = 2048
BRANCH = 256
LEAF = 256


EPS = 1e-06
ROPE_BASE = 1000000.0
INV_ROOT2 = 0.7071067811865476


def product(left, right):
    return jnp.dot(left, right, preferred_element_type=jnp.float32)


def product_nt(left, right):
    return lax.dot_general(
        left, right, (((1,), (1,)), ((), ())), preferred_element_type=jnp.float32
    )


def product_tn(left, right):
    return lax.dot_general(
        left, right, (((0,), (0,)), ((), ())), preferred_element_type=jnp.float32
    )


def rms_norm(vector, gain):
    return vector * lax.rsqrt(jnp.mean(vector * vector, axis=-1, keepdims=True) + EPS) * gain


def gelu_tanh(vector):
    return jax.nn.gelu(vector, approximate=True)


def rope_tables(places):
    index = jnp.arange(HD // 2, dtype=jnp.float32)
    freq = jnp.exp(index * (-2.0 * math.log(ROPE_BASE) / HD))
    angle = places.astype(jnp.float32)[:, None] * freq[None, :]
    return (jnp.cos(angle)[:, None, :], jnp.sin(angle)[:, None, :])


def rotate(vector, angle_cos, angle_sin):
    half = vector.shape[-1] // 2
    first = vector[..., :half]
    second = vector[..., half:]
    return jnp.concatenate(
        [first * angle_cos - second * angle_sin, second * angle_cos + first * angle_sin], axis=-1
    )


def head_prep(raw, gain, angle_cos, angle_sin):
    heads = raw.reshape(raw.shape[0], -1, gain.shape[0])
    return rotate(rms_norm(heads, gain), angle_cos, angle_sin)


def per_device(
    hidden_in,
    per_layer_in,
    cotangent,
    norm_in,
    w_query,
    w_key,
    w_value,
    query_norm,
    key_norm,
    w_out,
    post_attn_norm,
    laurel_left,
    laurel_right,
    laurel_norm,
    pre_ffn_norm,
    w_gate,
    w_up,
    w_down,
    post_ffn_norm,
    per_layer_gate,
    per_layer_proj,
    per_layer_norm,
    parents,
    segment,
    position,
):
    bf16 = jnp.bfloat16
    row_count = hidden_in.shape[0]
    head_width = query_norm.shape[0]
    row_devices = lax.axis_size("row")
    col_devices = lax.axis_size("col")
    leaf_index = lax.axis_index("leaf")
    row_index = lax.axis_index("row")
    col_index = lax.axis_index("col")
    block_rows = row_count * row_devices
    group_rows = block_rows * col_devices
    tree_length = TRUNK + 4 * BRANCH + 8 * LEAF
    local_heads = w_query.shape[1] // head_width
    key_width = w_key.shape[1]
    key_heads = key_width // head_width
    key_head = row_index * local_heads // (H // KV)
    score_scale = head_width ** (-0.5)
    own_ids = (
        (leaf_index * row_devices + row_index) * col_devices + col_index
    ) * row_count + jnp.arange(row_count, dtype=jnp.int32)
    block_local = jnp.arange(block_rows, dtype=jnp.int32)
    block_ids = (
        (leaf_index * row_devices + block_local // row_count) * col_devices + col_index
    ) * row_count + block_local % row_count
    tree_start = col_index * block_rows // tree_length * tree_length
    window_view = tree_start + jnp.arange(tree_length, dtype=jnp.int32)
    key_ids = (
        (leaf_index * row_devices + window_view % block_rows // row_count) * col_devices
        + window_view // block_rows
    ) * row_count + window_view % row_count
    key_segment = segment[key_ids]
    key_place = position[key_ids]
    query_segment = segment[block_ids]
    query_place = position[block_ids]
    first_parent = parents[query_segment]
    second_parent = parents[first_parent]
    visible = (
        (key_segment[None, :] == query_segment[:, None])
        | (key_segment[None, :] == first_parent[:, None])
        | (key_segment[None, :] == second_parent[:, None])
    ) & (key_place[None, :] <= query_place[:, None])
    stream_in = hidden_in.astype(jnp.float32)
    normed, in_back = jax.vjp(rms_norm, stream_in, norm_in)
    normed_b = normed.astype(bf16)
    gathered = lax.all_gather(normed_b, "row", axis=0, tiled=True)
    query_raw = product(gathered, w_query)
    key_cols = lax.dynamic_slice_in_dim(w_key, key_head * head_width, head_width, 1)
    value_cols = lax.dynamic_slice_in_dim(w_value, key_head * head_width, head_width, 1)
    key_raw = product(gathered, key_cols)
    value_raw = product(gathered, value_cols)
    block_cos, block_sin = rope_tables(query_place)

    def query_prep_fn(raw, gain):
        return head_prep(raw, gain, block_cos, block_sin)

    query_prep, query_back = jax.vjp(query_prep_fn, query_raw, query_norm)
    query_b = query_prep.astype(bf16)
    key_b = head_prep(key_raw, key_norm, block_cos, block_sin)[:, 0, :].astype(bf16)
    value_b = value_raw.astype(bf16)
    keys_all, values_all = (
        lax.all_gather(key_b, "col", axis=0, tiled=True),
        lax.all_gather(value_b, "col", axis=0, tiled=True),
    )
    keys_tree = lax.dynamic_slice_in_dim(keys_all, tree_start, tree_length, 0)
    values_tree = lax.dynamic_slice_in_dim(values_all, tree_start, tree_length, 0)
    head_outputs = []
    log_totals = []
    for head_index in range(local_heads):
        scores = product_nt(query_b[:, head_index, :], keys_tree) * score_scale
        scores = jnp.where(visible, scores, -1e30)
        row_top = jnp.max(scores, axis=1, keepdims=True)
        exp_scores = jnp.exp(scores - row_top)
        row_total = jnp.sum(exp_scores, axis=1, keepdims=True)
        weights = (exp_scores / row_total).astype(bf16)
        head_outputs.append(product(weights, values_tree))
        log_totals.append(row_top + jnp.log(row_total))
    attended_b = jnp.concatenate(head_outputs, axis=1).astype(bf16)
    attn_raw = lax.psum_scatter(product(attended_b, w_out), "row", scatter_dimension=0, tiled=True)
    laurel_mid_b = product(normed_b, laurel_left).astype(bf16)
    laurel_raw = product(laurel_mid_b, laurel_right)

    def mix_one(stream_zero, attn_part, normed_part, laurel_part, attn_gain, laurel_gain):
        return (
            stream_zero
            + rms_norm(attn_part, attn_gain)
            + normed_part
            + rms_norm(laurel_part, laurel_gain)
        ) * INV_ROOT2

    stream_one, mix_back = jax.vjp(
        mix_one, stream_in, attn_raw, normed, laurel_raw, post_attn_norm, laurel_norm
    )
    ffn_input, ffn_in_back = jax.vjp(rms_norm, stream_one, pre_ffn_norm)
    ffn_input_b = ffn_input.astype(bf16)
    ffn_gathered = lax.all_gather(ffn_input_b, "row", axis=0, tiled=True)
    gate_value = product(ffn_gathered, w_gate)
    up_value = product(ffn_gathered, w_up)
    gelu_gate, gelu_back = jax.vjp(gelu_tanh, gate_value)
    hidden_b = (gelu_gate * up_value).astype(bf16)
    ffn_raw = lax.psum_scatter(product(hidden_b, w_down), "row", scatter_dimension=0, tiled=True)

    def mix_two(stream_part, ffn_part, ffn_gain):
        return stream_part + rms_norm(ffn_part, ffn_gain)

    stream_two, two_back = jax.vjp(mix_two, stream_one, ffn_raw, post_ffn_norm)
    stream_two_b = stream_two.astype(bf16)
    side_pre = product(stream_two_b, per_layer_gate)
    side_input = per_layer_in.astype(jnp.float32)
    side_act, side_act_back = jax.vjp(gelu_tanh, side_pre)
    side_b = (side_act * side_input).astype(bf16)
    side_raw = product(side_b, per_layer_proj)

    def mix_three(stream_part, side_part, side_gain):
        return stream_part + rms_norm(side_part, side_gain)

    output, three_back = jax.vjp(mix_three, stream_two, side_raw, per_layer_norm)
    grad_out = cotangent.astype(jnp.float32)
    grad_two, grad_side_raw, per_layer_norm_grad = three_back(grad_out)
    grad_side_b = grad_side_raw.astype(bf16)
    per_layer_proj_grad = product_tn(side_b, grad_side_b)
    grad_side = product_nt(grad_side_b, per_layer_proj)
    per_layer_in_grad = grad_side * side_act
    grad_pre_b = side_act_back(grad_side * side_input)[0].astype(bf16)
    per_layer_gate_grad = product_tn(stream_two_b, grad_pre_b)
    grad_two = grad_two + product_nt(grad_pre_b, per_layer_gate)
    grad_one, grad_ffn_raw, post_ffn_norm_grad = two_back(grad_two)
    grad_ffn_b = grad_ffn_raw.astype(bf16)
    grad_ffn_rows = lax.all_gather(grad_ffn_b, "row", axis=0, tiled=True)
    grad_hidden = product_nt(grad_ffn_rows, w_down)
    w_down_grad = product_tn(hidden_b, grad_ffn_rows)
    grad_gate_b = gelu_back(grad_hidden * up_value)[0].astype(bf16)
    grad_up_b = (grad_hidden * gelu_gate).astype(bf16)
    w_gate_grad = product_tn(ffn_gathered, grad_gate_b)
    w_up_grad = product_tn(ffn_gathered, grad_up_b)
    grad_ffn_input = lax.psum_scatter(
        (product_nt(grad_gate_b, w_gate) + product_nt(grad_up_b, w_up)).astype(jnp.bfloat16),
        "row",
        scatter_dimension=0,
        tiled=True,
    ).astype(jnp.float32)
    grad_one_extra, pre_ffn_norm_grad = ffn_in_back(grad_ffn_input)
    grad_one = grad_one + grad_one_extra
    (
        grad_zero,
        grad_attn_raw,
        grad_normed,
        grad_laurel_raw,
        post_attn_norm_grad,
        laurel_norm_grad,
    ) = mix_back(grad_one)
    grad_laurel_b = grad_laurel_raw.astype(bf16)
    laurel_right_grad = product_tn(laurel_mid_b, grad_laurel_b)
    grad_mid_b = product_nt(grad_laurel_b, laurel_right).astype(bf16)
    laurel_left_grad = product_tn(normed_b, grad_mid_b)
    grad_normed = grad_normed + product_nt(grad_mid_b, laurel_left)
    grad_attn_b = grad_attn_raw.astype(bf16)
    grad_attn_rows = lax.all_gather(grad_attn_b, "row", axis=0, tiled=True)
    grad_vec_b = product_nt(grad_attn_rows, w_out).astype(bf16)
    w_out_grad = product_tn(attended_b, grad_attn_rows)
    grad_queries = []
    grad_keys = jnp.zeros((tree_length, head_width), jnp.float32)
    grad_values = jnp.zeros((tree_length, head_width), jnp.float32)
    for head_index in range(local_heads):
        query_head = query_b[:, head_index, :]
        grad_head = grad_vec_b[:, head_index * head_width : (head_index + 1) * head_width]
        scores = product_nt(query_head, keys_tree) * score_scale
        probs = jnp.where(visible, jnp.exp(scores - log_totals[head_index]), 0.0)
        probs_b = probs.astype(bf16)
        grad_probs = product_nt(grad_head, values_tree)
        centre = jnp.sum(probs * grad_probs, axis=1, keepdims=True)
        grad_scores_b = (probs * (grad_probs - centre)).astype(bf16)
        grad_queries.append(product(grad_scores_b, keys_tree) * score_scale)
        grad_keys = grad_keys + product_tn(grad_scores_b, query_head) * score_scale
        grad_values = grad_values + product_tn(probs_b, grad_head)
    grad_query_raw, query_norm_grad = query_back(jnp.stack(grad_queries, axis=1))
    grad_query_b = grad_query_raw.astype(bf16)
    w_query_grad = product_tn(gathered, grad_query_b)
    grad_normed_query = lax.psum_scatter(
        product_nt(grad_query_b, w_query).astype(jnp.bfloat16),
        "row",
        scatter_dimension=0,
        tiled=True,
    ).astype(jnp.float32)
    pair_tree = jnp.stack([grad_keys, grad_values], axis=1)
    pair_full = jnp.zeros((group_rows, 2, key_width), jnp.float32)
    pair_full = lax.dynamic_update_slice(
        pair_full, pair_tree, (tree_start, 0, key_head * head_width)
    )
    pair_full = pair_full.reshape(col_devices, row_devices, row_count, 2 * key_width)
    pair_full = jnp.transpose(pair_full, (1, 0, 2, 3)).reshape(group_rows, 2 * key_width)
    pair_own = lax.psum_scatter(pair_full, ("row", "col"), scatter_dimension=0, tiled=True)
    grad_key_own = pair_own[:, :key_width].reshape(row_count, key_heads, head_width)
    grad_value_b = pair_own[:, key_width:].astype(bf16)
    own_cos, own_sin = rope_tables(position[own_ids])

    def key_prep_fn(raw, gain):
        return head_prep(raw, gain, own_cos, own_sin)

    key_own_raw = product(normed_b, w_key)
    _, key_back = jax.vjp(key_prep_fn, key_own_raw, key_norm)
    grad_key_raw, key_norm_grad = key_back(grad_key_own)
    grad_key_b = grad_key_raw.astype(bf16)
    w_key_full = product_tn(normed_b, grad_key_b)
    w_value_full = product_tn(normed_b, grad_value_b)
    grad_normed = (
        grad_normed
        + grad_normed_query
        + product_nt(grad_key_b, w_key)
        + product_nt(grad_value_b, w_value)
    )
    grad_in_norm, norm_in_grad = in_back(grad_normed)
    input_grad = grad_zero + grad_in_norm
    query_shard, out_shard, gate_shard, up_shard, down_shard = (
        lax.psum_scatter(
            w_query_grad.astype(jnp.bfloat16), ("leaf", "col"), scatter_dimension=0, tiled=True
        ).astype(jnp.float32),
        lax.psum_scatter(
            w_out_grad.astype(jnp.bfloat16), ("leaf", "col"), scatter_dimension=1, tiled=True
        ).astype(jnp.float32),
        lax.psum_scatter(
            w_gate_grad.astype(jnp.bfloat16), ("leaf", "col"), scatter_dimension=0, tiled=True
        ).astype(jnp.float32),
        lax.psum_scatter(
            w_up_grad.astype(jnp.bfloat16), ("leaf", "col"), scatter_dimension=0, tiled=True
        ).astype(jnp.float32),
        lax.psum_scatter(
            w_down_grad.astype(jnp.bfloat16), ("leaf", "col"), scatter_dimension=1, tiled=True
        ).astype(jnp.float32),
    )
    summed = lax.psum(
        (
            w_key_full,
            w_value_full,
            laurel_left_grad,
            laurel_right_grad,
            per_layer_gate_grad,
            per_layer_proj_grad,
            norm_in_grad,
            query_norm_grad,
            key_norm_grad,
            post_attn_norm_grad,
            laurel_norm_grad,
            pre_ffn_norm_grad,
            post_ffn_norm_grad,
            per_layer_norm_grad,
        ),
        ("leaf", "row", "col"),
    )
    quarter = key_width // row_devices
    key_grad_part = lax.dynamic_slice_in_dim(summed[0], row_index * quarter, quarter, 1)
    value_grad_part = lax.dynamic_slice_in_dim(summed[1], row_index * quarter, quarter, 1)
    return (
        output,
        input_grad,
        per_layer_in_grad,
        summed[6],
        query_shard,
        key_grad_part,
        value_grad_part,
        summed[7],
        summed[8],
        out_shard,
        summed[9],
        summed[2],
        summed[3],
        summed[10],
        summed[11],
        gate_shard,
        up_shard,
        down_shard,
        summed[12],
        summed[4],
        summed[5],
        summed[13],
    )


def solution(mesh):
    in_specs = (
        P(("leaf", "row", "col"), None),
        P(("leaf", "row", "col"), None),
        P(("leaf", "row", "col"), None),
        P(),
        P(None, "row"),
        P(),
        P(),
        P(),
        P(),
        P("row", None),
        P(),
        P(),
        P(),
        P(),
        P(),
        P(None, "row"),
        P(None, "row"),
        P("row", None),
        P(),
        P(),
        P(),
        P(),
        P(),
        P(),
        P(),
    )
    out_specs = (
        P(("leaf", "row", "col"), None),
        P(("leaf", "row", "col"), None),
        P(("leaf", "row", "col"), None),
        P(),
        P(("leaf", "col"), "row"),
        P(None, "row"),
        P(None, "row"),
        P(),
        P(),
        P("row", ("leaf", "col")),
        P(),
        P(),
        P(),
        P(),
        P(),
        P(("leaf", "col"), "row"),
        P(("leaf", "col"), "row"),
        P("row", ("leaf", "col")),
        P(),
        P(),
        P(),
        P(),
    )
    return jax.shard_map(
        per_device, mesh=mesh, in_specs=in_specs, out_specs=out_specs, check_vma=False
    )
```

profile of v0, /device:TPU:0, one launch (start us, length us, event | category | flops | bytes accessed | tf_op | source)
XLA Modules:
  0.0 2581.2 jit_solution(6949860801844155167)
XLA Ops:
  27.4 86.5 %all-gather.8.cloned.1.call-done = bf16[1280,2048]{1,0:T(8,128)(2,1)} async-done(((bf16[320,2048]{1,0:T(8,128)(2,1)}), bf16[1280,2048]{1,0:T(8,128)(2,1)}) %all-gather.8.cloned.1.call-update) | async-done | bytes 5242896 | tf_op jit(solution)/shard_map/all_gather | solution.py:136
  123.0 28.7 %gather_fusion.2 = s32[5120]{0:T(1024)S(1)} fusion(s32[10240]{0:T(1024)S(1)} %copy-done.1, s32[5120]{0:T(1024)S(1)} %broadcast_clamp_fusion), kind=kCustom, calls=%fused_computation.2 | custom fusion | bytes 61440 | tf_op jit(solution)/shard_map/gather | solution.py:123
  151.7 28.7 %gather_fusion = s32[5120]{0:T(1024)S(1)} fusion(s32[10240]{0:T(1024)S(1)} %copy-done.3, s32[5120]{0:T(1024)S(1)} %broadcast_clamp_fusion), kind=kCustom, calls=%fused_computation | custom fusion | bytes 61440 | tf_op jit(solution)/shard_map/gather | solution.py:122
  335.4 168.8 %reduce-scatter.11.cloned.1.call-done = f32[320,2048]{1,0:T(8,128)} async-done(((f32[1280,2048]{1,0:T(8,128)}), f32[320,2048]{1,0:T(8,128)}) %reduce-scatter.11.cloned.1.call-update) | async-done | bytes 2621456 | tf_op jit(solution)/shard_map/reduce_scatter | solution.py:169
  513.5 99.2 %all-gather.12.cloned.1.call-done = bf16[1280,2048]{1,0:T(8,128)(2,1)} async-done(((bf16[320,2048]{1,0:T(8,128)(2,1)}), bf16[1280,2048]{1,0:T(8,128)(2,1)}) %all-gather.12.cloned.1.call-update) | async-done | bytes 5242896 | tf_op jit(solution)/shard_map/all_gather | solution.py:186
  630.7 21.6 multiply_convert_fusion.3
  667.2 176.5 %reduce-scatter.13.cloned.1.call-done = f32[320,2048]{1,0:T(8,128)} async-done(((f32[1280,2048]{1,0:T(8,128)}), f32[320,2048]{1,0:T(8,128)}) %reduce-scatter.13.cloned.1.call-update) | async-done | bytes 2621456 | tf_op jit(solution)/shard_map/reduce_scatter | solution.py:191
  863.7 99.2 %all-gather.14.cloned.1.call-done = bf16[1280,2048]{1,0:T(8,128)(2,1)} async-done(((bf16[320,2048]{1,0:T(8,128)(2,1)}), bf16[1280,2048]{1,0:T(8,128)(2,1)}) %all-gather.14.cloned.1.call-update) | async-done | bytes 5242896 | tf_op jit(solution)/shard_map/all_gather | solution.py:219
  962.8 29.0 %multiply_convert_fusion.2 = (bf16[1280,2048]{1,0:T(8,128)(2,1)}, bf16[1280,2048]{1,0:T(8,128)(2,1)}) fusion(f32[1280,2048]{1,0:T(8,128)} %fusion.137, f32[1280,2048]{1,0:T(8,128)} %get-tuple-element.163, bf16[1280,2048]{1,0:T(8,128)(2,1)} %all-gather.14.cloned.1.call-done, bf16[2048,2048]{1,0:T(8,128)(2,1)} %param.42), kind=kOutput, calls=%fused_computation.40 | convolution fusion | flops 10800332800 | bytes 45088768 | tf_op jit(solution)/shard_map/dot_general | solution.py:26
  1024.5 91.6 %reduce-scatter.15.cloned.1.call-done = bf16[320,2048]{1,0:T(8,128)(2,1)} async-done(((bf16[1280,2048]{1,0:T(8,128)(2,1)}), bf16[320,2048]{1,0:T(8,128)(2,1)}) %reduce-scatter.15.cloned.1.call-update) | async-done | bytes 1310736 | tf_op jit(solution)/shard_map/reduce_scatter | solution.py:226
  1129.0 98.5 %all-gather.16.cloned.1.call-done = bf16[1280,2048]{1,0:T(8,128)(2,1)} async-done(((bf16[320,2048]{1,0:T(8,128)(2,1)}), bf16[1280,2048]{1,0:T(8,128)(2,1)}) %all-gather.16.cloned.1.call-update) | async-done | bytes 5242896 | tf_op jit(solution)/shard_map/all_gather | solution.py:248
  1283.4 38.2 %multiply_reduce_fusion.1 = (f32[1280]{0:T(1024)S(1)}, f32[1280]{0:T(1024)S(1)}, f32[1280,5120]{1,0:T(8,128)}) fusion(f32[1280]{0:T(1024)S(1)} %get-tuple-element.170, f32[1280,5120]{1,0:T(8,128)} %get-tuple-element.160, s32[1280]{0:T(1024)S(1)} %copy-done.74, s32[5120]{0:T(1024)S(1)} %copy-done.62, s32[1280]{0:T(1024)S(1)} %copy-done.79, ...), kind=kOutput, calls=%fused_computation.9 | convolution fusion | flops 3466851840 | bytes 108216320 | tf_op jit(solution)/shard_map/dot_general | solution.py:26
  1321.6 44.8 %multiply_convert_fusion.1 = (bf16[1280,5120]{1,0:T(8,128)(2,1)}, bf16[1280,5120]{1,0:T(8,128)(2,1)}) fusion(f32[1280,5120]{1,0:T(8,128)} %get-tuple-element.167, f32[1280]{0:T(1024)S(1)} %get-tuple-element.40, f32[1280]{0:T(1024)S(1)} %get-tuple-element.170, f32[1280,5120]{1,0:T(8,128)} %get-tuple-element.160, s32[1280]{0:T(1024)S(1)} %copy-done.74, ...), kind=kLoop, calls=%fused_computation.8 | loop fusion | flops 124518400 | bytes 131153920 | tf_op jit(solution)/shard_map/convert_element_type | solution.py:262
  1393.1 29.1 %copy_dynamic-update-slice_fusion = f32[5120,2,512]{2,1,0:T(2,128)} fusion(f32[5120,2,512]{2,1,0:T(2,128)} %broadcast_in_dim.32, s32[]{:T(128)S(6)} %select_n.168, f32[5120,2,256]{2,0,1:T(8,128)S(1)} %pad_maximum_fusion), kind=kLoop, calls=%fused_computation.38 | loop fusion | bytes 20971524 | tf_op jit(solution)/shard_map/dynamic_update_slice | solution.py:277
  1422.1 27.3 %reshape.645 = f32[4,4,320,1024]{3,2,1,0:T(8,128)} reshape(f32[5120,2,512]{2,1,0:T(2,128)} %copy_dynamic-update-slice_fusion) | data formatting | bytes 41943040 | tf_op jit(solution)/shard_map/reshape | solution.py:280
  1577.5 317.7 %reduce-scatter.19.cloned.1.call-done = f32[320,1024]{1,0:T(8,128)} async-done(((f32[5120,1024]{1,0:T(8,128)}), f32[320,1024]{1,0:T(8,128)}) %reduce-scatter.19.cloned.1.call-update) | async-done | bytes 1310736 | tf_op jit(solution)/shard_map/reduce_scatter | solution.py:282
  1916.2 60.1 %reduce-scatter.29.cloned.1.call-done = bf16[2048,256]{1,0:T(8,128)(2,1)} async-done(((bf16[2048,2048]{1,0:T(8,128)(2,1)}), bf16[2048,256]{1,0:T(8,128)(2,1)}) %reduce-scatter.29.cloned.1.call-update) | async-done | bytes 1048592 | tf_op jit(solution)/shard_map/reduce_scatter | solution.py:317
  1979.1 72.1 %reduce-scatter.27.cloned.1.call-done = bf16[256,2048]{1,0:T(8,128)(2,1)} async-done(((bf16[2048,2048]{1,0:T(8,128)(2,1)}), bf16[256,2048]{1,0:T(8,128)(2,1)}) %reduce-scatter.27.cloned.1.call-update) | async-done | bytes 1048592 | tf_op jit(solution)/shard_map/reduce_scatter | solution.py:314
  2054.0 72.2 %reduce-scatter.25.cloned.1.call-done = bf16[256,2048]{1,0:T(8,128)(2,1)} async-done(((bf16[2048,2048]{1,0:T(8,128)(2,1)}), bf16[256,2048]{1,0:T(8,128)(2,1)}) %reduce-scatter.25.cloned.1.call-update) | async-done | bytes 1048592 | tf_op jit(solution)/shard_map/reduce_scatter | solution.py:311
  2129.0 42.1 %reduce-scatter.23.cloned.1.call-done = bf16[512,256]{1,0:T(8,128)(2,1)} async-done(((bf16[512,2048]{1,0:T(8,128)(2,1)}), bf16[512,256]{1,0:T(8,128)(2,1)}) %reduce-scatter.23.cloned.1.call-update) | async-done | bytes 262160 | tf_op jit(solution)/shard_map/reduce_scatter | solution.py:308
  2172.8 43.1 %reduce-scatter.21.cloned.1.call-done = bf16[256,512]{1,0:T(8,128)(2,1)} async-done(((bf16[2048,512]{1,0:T(8,128)(2,1)}), bf16[256,512]{1,0:T(8,128)(2,1)}) %reduce-scatter.21.cloned.1.call-update) | async-done | bytes 262160 | tf_op jit(solution)/shard_map/reduce_scatter | solution.py:305
  2217.7 94.1 %reduce-scatter.17.cloned.1.call-done = bf16[320,2048]{1,0:T(8,128)(2,1)} async-done(((bf16[1280,2048]{1,0:T(8,128)(2,1)}), bf16[320,2048]{1,0:T(8,128)(2,1)}) %reduce-scatter.17.cloned.1.call-update) | async-done | bytes 1310736 | tf_op jit(solution)/shard_map/reduce_scatter | solution.py:269
  2319.9 43.9 %all-reduce.4 = (f32[2048]{0:T(1024)}, f32[256]{0:T(256)}, f32[256]{0:T(256)}, f32[2048]{0:T(1024)}, f32[2048]{0:T(1024)}, /*index=5*/f32[2048]{0:T(1024)}, f32[2048]{0:T(1024)}, f32[2048]{0:T(1024)}) all-reduce(f32[2048]{0:T(1024)S(1)} %get-tuple-element.32, ...), channel_id=1, replica_groups=mesh['leaf'=2,'row'=4,'col'=4] {'leaf','row','col'}, use_global_device_ids=true, to_apply=%region_29.30 | all-reduce | flops 12800 | bytes 102400 | tf_op jit(solution)/shard_map/psum | solution.py:321
  2368.7 196.8 %all-reduce.8.cloned.1.call-done = (f32[2048,512]{1,0:T(8,128)}, f32[2048,512]{1,0:T(8,128)}, f32[2048,64]{0,1:T(8,128)}, f32[64,2048]{1,0:T(8,128)}, f32[2048,256]{1,0:T(8,128)}, /*index=5*/f32[256,2048]{1,0:T(8,128)}) async-done(((f32[2048,512]{1,0:T(8,128)}, f32[2048,512]{1,0:T(8,128)}, f32[2048,64]{0,1:T(8,128)}, f32[64,2048]{1,0:T(8,128)}, f32[2048,256]{1,0:T(8,128)}, ...) | async-done | bytes 13631504 | tf_op jit(solution)/shard_map/psum | solution.py:321
  (457 shorter events, 555.8 us)
Async XLA Ops:
  7.2 211.0 %copy-start = (bf16[2048,512]{1,0:T(8,128)(2,1)S(1)}, bf16[2048,512]{1,0:T(8,128)(2,1)}, u32[]{:S(2)}) copy-start(bf16[2048,512]{1,0:T(8,128)(2,1)} %param.29) | copy-start | bytes 6291460
  7.2 106.7 %all-gather.8.cloned.1.call-start = ((), (), s32[]{:S(2)}) async-start(), calls=%async_computation.10 | async-start | bytes 6553600 | tf_op jit(solution)/shard_map/all_gather | solution.py:136
  13.0 219.5 %all-gather.18.cloned.1.call-start = ((), (), s32[]{:S(2)}) async-start(), calls=%async_computation.25 | async-start | bytes 3276800 | tf_op jit(solution)/shard_map/all_gather | solution.py:152
  20.2 285.1 %copy-start.73 = (s32[1280]{0:T(1024)}, s32[1280]{0:T(1024)S(1)}, u32[]{:S(2)}) copy-start(s32[1280]{0:T(1024)S(1)} %gather_fusion.3) | copy-start | bytes 15364
  27.3 278.0 %copy-start.71 = (s32[1280]{0:T(1024)}, s32[1280]{0:T(1024)S(1)}, u32[]{:S(2)}) copy-start(s32[1280]{0:T(1024)S(1)} %gather_fusion.1) | copy-start | bytes 15364
  27.4 188.4 %copy-start.122 = (f32[128]{0:T(128)}, f32[128]{0:T(128)S(1)}, u32[]{:S(2)}) copy-start(f32[128]{0:T(128)S(1)} %multiply_exponential_fusion) | copy-start | bytes 1540
  122.1 165.3 %all-gather.10.cloned.1.call-start = ((), (), s32[]{:S(2)}) async-start(), calls=%async_computation.11 | async-start | bytes 3276800 | tf_op jit(solution)/shard_map/all_gather | solution.py:153
  228.8 275.4 %reduce-scatter.11.cloned.1.call-start = ((), (), s32[]{:S(2)}) async-start(), calls=%async_computation.12 | async-start | bytes 13107200 | tf_op jit(solution)/shard_map/reduce_scatter | solution.py:169
  328.3 284.5 %all-gather.12.cloned.1.call-start = ((), (), s32[]{:S(2)}) async-start(), calls=%async_computation.13 | async-start | bytes 6553600 | tf_op jit(solution)/shard_map/all_gather | solution.py:186
  513.5 330.2 %reduce-scatter.13.cloned.1.call-start = ((), (), s32[]{:S(2)}) async-start(), calls=%async_computation.14 | async-start | bytes 13107200 | tf_op jit(solution)/shard_map/reduce_scatter | solution.py:191
  667.1 178.7 %copy-start.77 = (f32[2048]{0:T(1024)S(1)}, f32[2048]{0:T(1024)}, u32[]{:S(2)}) copy-start(f32[2048]{0:T(1024)} %param.43) | copy-start | bytes 24580
  667.2 295.7 %all-gather.14.cloned.1.call-start = ((), (), s32[]{:S(2)}) async-start(), calls=%async_computation.15 | async-start | bytes 6553600 | tf_op jit(solution)/shard_map/all_gather | solution.py:219
  863.6 252.5 %reduce-scatter.15.cloned.1.call-start = ((), (), s32[]{:S(2)}) async-start(), calls=%async_computation.16 | async-start | bytes 6553600 | tf_op jit(solution)/shard_map/reduce_scatter | solution.py:226
  1023.9 203.6 %all-gather.16.cloned.1.call-start = ((), (), s32[]{:S(2)}) async-start(), calls=%async_computation.17 | async-start | bytes 6553600 | tf_op jit(solution)/shard_map/all_gather | solution.py:248
  1128.8 766.3 %reduce-scatter.19.cloned.1.call-start = ((), (), s32[]{:S(2)}) async-start(), calls=%async_computation.19 | async-start | bytes 22282240 | tf_op jit(solution)/shard_map/reduce_scatter | solution.py:282
  1465.8 510.6 %reduce-scatter.29.cloned.1.call-start = ((), (), s32[]{:S(2)}) async-start(), calls=%async_computation.24 | async-start | bytes 9437184 | tf_op jit(solution)/shard_map/reduce_scatter | solution.py:317
  1482.7 568.5 %reduce-scatter.27.cloned.1.call-start = ((), (), s32[]{:S(2)}) async-start(), calls=%async_computation.23 | async-start | bytes 9437184 | tf_op jit(solution)/shard_map/reduce_scatter | solution.py:314
  1499.5 626.7 %reduce-scatter.25.cloned.1.call-start = ((), (), s32[]{:S(2)}) async-start(), calls=%async_computation.22 | async-start | bytes 9437184 | tf_op jit(solution)/shard_map/reduce_scatter | solution.py:311
  1516.5 654.6 %reduce-scatter.23.cloned.1.call-start = ((), (), s32[]{:S(2)}) async-start(), calls=%async_computation.21 | async-start | bytes 2359296 | tf_op jit(solution)/shard_map/reduce_scatter | solution.py:308
  1524.7 691.2 %reduce-scatter.21.cloned.1.call-start = ((), (), s32[]{:S(2)}) async-start(), calls=%async_computation.20 | async-start | bytes 2359296 | tf_op jit(solution)/shard_map/reduce_scatter | solution.py:305
  1549.8 762.0 %reduce-scatter.17.cloned.1.call-start = ((), (), s32[]{:S(2)}) async-start(), calls=%async_computation.18 | async-start | bytes 6553600 | tf_op jit(solution)/shard_map/reduce_scatter | solution.py:269
  1554.6 1010.9 %all-reduce.8.cloned.1.call-start = ((), (), s32[]{:S(2)}) async-start(), calls=%async_computation.26 | async-start | bytes 27262976 | tf_op jit(solution)/shard_map/psum | solution.py:321
  1576.3 325.4 %copy-start.114 = (f32[256]{0:T(256)S(1)}, f32[256]{0:T(256)}, u32[]{:S(2)}) copy-start(f32[256]{0:T(256)} %param.33) | copy-start | bytes 3076
  2054.0 257.8 %copy-start.48 = (bf16[2048,64]{0,1:T(8,128)(2,1)S(1)}, bf16[2048,64]{0,1:T(8,128)(2,1)}, u32[]{:S(2)}) copy-start(bf16[2048,64]{0,1:T(8,128)(2,1)} %param.36) | copy-start | bytes 786436
  (135 other events, 3718.9 us)
Sparse Core Ops, SparseCore 0:
  13.1 100.7 all-gather.7
  122.2 37.8 all-gather.17
  228.9 37.8 all-gather.9
  328.4 175.7 reduce-scatter.10
  513.6 99.0 all-gather.11
  667.3 176.3 reduce-scatter.12
  863.7 99.0 all-gather.13
  1023.9 92.1 reduce-scatter.14
  1128.9 98.5 all-gather.15
  1465.9 429.1 reduce-scatter.18
  1898.6 77.7 reduce-scatter.28
  1979.7 71.4 reduce-scatter.26
  2054.7 71.4 reduce-scatter.24
  2129.9 41.0 reduce-scatter.22
  2174.7 41.0 reduce-scatter.20
  2218.0 93.7 reduce-scatter.16
  2319.2 246.2 all-reduce.7
where the time goes:
time: 2590 us; the launch traced here: 2580 us
  waiting for transfers between devices  1720 us (66%)
  matrix products  429 us (17%)
  local copies, waits for them, and re-layouts  204 us (8%)
  other arithmetic  168 us (6%)
  blocking collectives  43.9 us (2%)
    reduce_scatter x1, waiting for transfers between devices, per_device(): lax.psum_scatter(pair_full, ('row', 'col'), scatter_dimension=0, tiled=True)  318 us
    psum x1, waiting for transfers between devices, per_device(): lax.psum((w_key_full, w_value_full, laurel_left_grad, laurel_right_grad,...  197 us
    reduce_scatter x1, waiting for transfers between devices, per_device(): lax.psum_scatter(product(hidden_b, w_down), 'row', scatter_dimension=0, t...  176 us
    reduce_scatter x1, waiting for transfers between devices, per_device(): lax.psum_scatter(product(attended_b, w_out), 'row', scatter_dimension=0,...  169 us
    dot_general x15, matrix products, product_nt(): lax.dot_general(left, right, (((1,), (1,)), ((), ())), preferred_element_...  167 us
    dot_general x16, matrix products, product(): return jnp.dot(left, right, preferred_element_type=jnp.float32)  135 us
    dot_general x15, matrix products, product_tn(): lax.dot_general(left, right, (((0,), (0,)), ((), ())), preferred_element_...  127 us
    all_gather x1, waiting for transfers between devices, per_device(): ffn_gathered = lax.all_gather(ffn_input_b, 'row', axis=0, tiled=True)  99.2 us
  transfers between devices with their start and end apart: 17, of which 15 were waited for; matrix products, arithmetic and copies ran while one was open for 13% of the time, Pallas kernels for 0%

commit v1 on v0

v1 whole, which is shorter than its diff:
```python
import functools
import math

import jax
import jax.numpy as jnp
from jax import lax
from jax.experimental import pallas as pl
from jax.experimental.pallas import tpu as pltpu
from jax.sharding import PartitionSpec as P

H = 8
KV = 2
HD = 256
TRUNK = 2048
BRANCH = 256
LEAF = 256
KEY_BLOCK = 256
GROUP = H // KV
LOG2E = 1.4426950408889634


EPS = 1e-06
ROPE_BASE = 1000000.0
INV_ROOT2 = 0.7071067811865476


def product(left, right):
    return jnp.dot(left, right, preferred_element_type=jnp.float32)


def product_nt(left, right):
    return lax.dot_general(
        left, right, (((1,), (1,)), ((), ())), preferred_element_type=jnp.float32
    )


def product_tn(left, right):
    return lax.dot_general(
        left, right, (((0,), (0,)), ((), ())), preferred_element_type=jnp.float32
    )


def rms_norm(vector, gain):
    return vector * lax.rsqrt(jnp.mean(vector * vector, axis=-1, keepdims=True) + EPS) * gain


def gelu_tanh(vector):
    return jax.nn.gelu(vector, approximate=True)


def rope_tables(places):
    index = jnp.arange(HD // 2, dtype=jnp.float32)
    freq = jnp.exp(index * (-2.0 * math.log(ROPE_BASE) / HD))
    angle = places.astype(jnp.float32)[:, None] * freq[None, :]
    return (jnp.cos(angle)[:, None, :], jnp.sin(angle)[:, None, :])


def rotate(vector, angle_cos, angle_sin):
    half = vector.shape[-1] // 2
    first = vector[..., :half]
    second = vector[..., half:]
    return jnp.concatenate(
        [first * angle_cos - second * angle_sin, second * angle_cos + first * angle_sin], axis=-1
    )


def head_prep(raw, gain, angle_cos, angle_sin):
    heads = raw.reshape(raw.shape[0], -1, gain.shape[0])
    return rotate(rms_norm(heads, gain), angle_cos, angle_sin)


def head_rows(ref, kv_head, head_width):
    base = kv_head * GROUP * head_width
    return jnp.concatenate(
        [ref[:, base + g * head_width : base + (g + 1) * head_width] for g in range(GROUP)], axis=0
    )


def attend_kernel(scale, key_heads, idx, count, own, offset, q_ref, kv_ref, o_ref, lse_ref, acc, den):
    step = pl.program_id(0)
    sub = q_ref.shape[0]
    width = q_ref.shape[1] // (key_heads * GROUP)
    rows = GROUP * sub
    queries = [head_rows(q_ref, h, width) for h in range(key_heads)]

    def block(start, mask):
        for h in range(key_heads):
            keys = kv_ref[pl.ds(start, KEY_BLOCK), h * width : (h + 1) * width]
            values = kv_ref[pl.ds(start, KEY_BLOCK), (key_heads + h) * width : (key_heads + h + 1) * width]
            weights = jnp.exp2(product_nt(queries[h], keys) * (scale * LOG2E))
            if mask is not None:
                weights = jnp.where(mask, weights, 0.0)
            part = product(weights.astype(jnp.bfloat16), values)
            if mask is not None:
                acc[h] = part
                den[h] = weights
            else:
                acc[h] += part
                den[h] += weights

    token = offset[step] + lax.broadcasted_iota(jnp.int32, (rows, KEY_BLOCK), 0) % sub
    place = lax.broadcasted_iota(jnp.int32, (rows, KEY_BLOCK), 1)
    block(pl.multiple_of(own[step] * KEY_BLOCK, KEY_BLOCK), place <= token)

    def body(j, carry):
        block(pl.multiple_of(idx[step, j] * KEY_BLOCK, KEY_BLOCK), None)
        return carry

    lax.fori_loop(0, count[step], body, 0)
    for h in range(key_heads):
        total = jnp.sum(den[h], axis=1, keepdims=True)
        result = (acc[h] / total).astype(jnp.bfloat16)
        for g in range(GROUP):
            at = (h * GROUP + g) * width
            o_ref[:, at : at + width] = result[g * sub : (g + 1) * sub]
        lse_ref[0, h] = jnp.transpose(jnp.broadcast_to(jnp.log2(total), (rows, 128)))[:8]


def attend_back_kernel(
    scale, key_heads, idx, count, own, offset, q_ref, d_ref, lse_ref, mid_ref, kv_ref, dq_ref, dkv_ref, acc, dq
):
    step = pl.program_id(0)
    sub = q_ref.shape[0]
    width = q_ref.shape[1] // (key_heads * GROUP)
    rows = GROUP * sub
    queries = [head_rows(q_ref, h, width) for h in range(key_heads)]
    grads = [head_rows(d_ref, h, width) for h in range(key_heads)]

    @pl.when(step == 0)
    def _():
        acc[...] = jnp.zeros_like(acc)

    def block(start, mask):
        for h in range(key_heads):
            k_at = slice(h * width, (h + 1) * width)
            v_at = slice((key_heads + h) * width, (key_heads + h + 1) * width)
            keys = kv_ref[pl.ds(start, KEY_BLOCK), k_at]
            values = kv_ref[pl.ds(start, KEY_BLOCK), v_at]
            weights = jnp.exp2(product_nt(keys, queries[h]) * (scale * LOG2E) - lse_ref[0, h, :1])
            if mask is not None:
                weights = jnp.where(mask, weights, 0.0)
            slopes = (weights * (product_nt(values, grads[h]) - mid_ref[0, h, :1])).astype(jnp.bfloat16)
            acc[pl.ds(start, KEY_BLOCK), v_at] += product(weights.astype(jnp.bfloat16), grads[h])
            acc[pl.ds(start, KEY_BLOCK), k_at] += product(slopes, queries[h])
            part = product_tn(slopes, keys)
            if mask is not None:
                dq[h] = part
            else:
                dq[h] += part

    token = offset[step] + lax.broadcasted_iota(jnp.int32, (KEY_BLOCK, rows), 1) % sub
    place = lax.broadcasted_iota(jnp.int32, (KEY_BLOCK, rows), 0)
    block(pl.multiple_of(own[step] * KEY_BLOCK, KEY_BLOCK), place <= token)

    def body(j, carry):
        block(pl.multiple_of(idx[step, j] * KEY_BLOCK, KEY_BLOCK), None)
        return carry

    lax.fori_loop(0, count[step], body, 0)
    for h in range(key_heads):
        for g in range(GROUP):
            at = (h * GROUP + g) * width
            dq_ref[:, at : at + width] = dq[h, g * sub : (g + 1) * sub] * scale

    @pl.when(step == pl.num_programs(0) - 1)
    def _():
        half = key_heads * width

        def out(j, carry):
            at = pl.ds(pl.multiple_of(j * KEY_BLOCK, KEY_BLOCK), KEY_BLOCK)
            dkv_ref[at, :half] = (acc[at, :half] * scale).astype(jnp.bfloat16)
            dkv_ref[at, half:] = acc[at, half:].astype(jnp.bfloat16)
            return carry

        lax.fori_loop(0, acc.shape[0] // KEY_BLOCK, out, 0)


def attend(plan, query_b, kv_tree, sub):
    tokens, total = query_b.shape
    key_heads = KV
    width = total // H
    steps = tokens // sub
    rows = GROUP * sub
    return pl.pallas_call(
        functools.partial(attend_kernel, width ** (-0.5), key_heads),
        out_shape=(
            jax.ShapeDtypeStruct((tokens, total), jnp.bfloat16),
            jax.ShapeDtypeStruct((steps, key_heads, 8, rows), jnp.float32),
        ),
        grid_spec=pltpu.PrefetchScalarGridSpec(
            num_scalar_prefetch=4,
            grid=(steps,),
            in_specs=[
                pl.BlockSpec((sub, total), lambda i, *_: (i, 0)),
                pl.BlockSpec(kv_tree.shape, lambda i, *_: (0, 0), pipeline_mode=pl.Buffered(1)),
            ],
            out_specs=[
                pl.BlockSpec((sub, total), lambda i, *_: (i, 0)),
                pl.BlockSpec((1, key_heads, 8, rows), lambda i, *_: (i, 0, 0, 0)),
            ],
            scratch_shapes=[
                pltpu.VMEM((key_heads, rows, width), jnp.float32),
                pltpu.VMEM((key_heads, rows, KEY_BLOCK), jnp.float32),
            ],
        ),
        compiler_params=pltpu.CompilerParams(vmem_limit_bytes=48 * 1024 * 1024),
        name="attend",
    )(*plan, query_b, kv_tree)


def attend_back(plan, query_b, grad_b, lse, middle, kv_tree, sub):
    tokens, total = query_b.shape
    key_heads = KV
    width = total // H
    steps = tokens // sub
    rows = GROUP * sub
    return pl.pallas_call(
        functools.partial(attend_back_kernel, width ** (-0.5), key_heads),
        out_shape=(
            jax.ShapeDtypeStruct((tokens, total), jnp.float32),
            jax.ShapeDtypeStruct(kv_tree.shape, jnp.bfloat16),
        ),
        grid_spec=pltpu.PrefetchScalarGridSpec(
            num_scalar_prefetch=4,
            grid=(steps,),
            in_specs=[
                pl.BlockSpec((sub, total), lambda i, *_: (i, 0)),
                pl.BlockSpec((sub, total), lambda i, *_: (i, 0)),
                pl.BlockSpec((1, key_heads, 8, rows), lambda i, *_: (i, 0, 0, 0)),
                pl.BlockSpec((1, key_heads, 1, rows), lambda i, *_: (i, 0, 0, 0)),
                pl.BlockSpec(kv_tree.shape, lambda i, *_: (0, 0), pipeline_mode=pl.Buffered(1)),
            ],
            out_specs=[
                pl.BlockSpec((sub, total), lambda i, *_: (i, 0)),
                pl.BlockSpec(kv_tree.shape, lambda i, *_: (0, 0), pipeline_mode=pl.Buffered(1)),
            ],
            scratch_shapes=[
                pltpu.VMEM(kv_tree.shape, jnp.float32),
                pltpu.VMEM((key_heads, rows, width), jnp.float32),
            ],
        ),
        compiler_params=pltpu.CompilerParams(vmem_limit_bytes=60 * 1024 * 1024),
        name="attend_back",
    )(*plan, query_b, grad_b, lse, middle, kv_tree)


def key_plan(parents, segment, position, rows, view_start, tree_start, tree_length, sub, leaf, sizes):
    leaf_devices, row_devices, col_devices = sizes

    def blocks(values):
        grid = values.reshape(leaf_devices, row_devices, col_devices, rows)
        mine = lax.dynamic_index_in_dim(grid, leaf, 0, keepdims=False)
        view = jnp.transpose(mine, (1, 0, 2)).reshape(-1, KEY_BLOCK)[:, 0]
        return lax.dynamic_slice_in_dim(view, tree_start // KEY_BLOCK, tree_length // KEY_BLOCK)

    def pick(table, index):
        at = jnp.arange(table.shape[0], dtype=jnp.int32)
        return jnp.sum(jnp.where(index[:, None] == at[None, :], table[None, :], 0), axis=1)

    block_segment = blocks(segment)
    block_place = blocks(position)
    begin = view_start - tree_start + sub * jnp.arange(rows // sub, dtype=jnp.int32)
    own = begin // KEY_BLOCK
    offset = begin % KEY_BLOCK
    query_segment = pick(block_segment, own)
    query_place = pick(block_place, own) + offset
    first = pick(parents, query_segment)
    second = pick(parents, first)
    number = jnp.arange(tree_length // KEY_BLOCK, dtype=jnp.int32)
    seen = (
        (block_segment[None, :] == query_segment[:, None])
        | (block_segment[None, :] == first[:, None])
        | (block_segment[None, :] == second[:, None])
    )
    seen = seen & (block_place[None, :] <= query_place[:, None]) & (number[None, :] != own[:, None])
    flags = seen.astype(jnp.int32)
    before = number[:, None] < number[None, :]
    rank = jnp.sum(jnp.where(before[None], flags[:, :, None], 0), axis=1)
    slot = (rank[:, None, :] == number[None, :, None]) & seen[:, None, :]
    idx = jnp.sum(jnp.where(slot, number[None, None, :], 0), axis=2)
    return idx, jnp.sum(flags, axis=1), own, offset


def per_device(
    hidden_in,
    per_layer_in,
    cotangent,
    norm_in,
    w_query,
    w_key,
    w_value,
    query_norm,
    key_norm,
    w_out,
    post_attn_norm,
    laurel_left,
    laurel_right,
    laurel_norm,
    pre_ffn_norm,
    w_gate,
    w_up,
    w_down,
    post_ffn_norm,
    per_layer_gate,
    per_layer_proj,
    per_layer_norm,
    parents,
    segment,
    position,
):
    bf16 = jnp.bfloat16
    row_count = hidden_in.shape[0]
    head_width = query_norm.shape[0]
    row_devices = lax.axis_size("row")
    col_devices = lax.axis_size("col")
    leaf_index = lax.axis_index("leaf")
    row_index = lax.axis_index("row")
    col_index = lax.axis_index("col")
    block_rows = row_count * row_devices
    group_rows = block_rows * col_devices
    tree_length = TRUNK + 4 * BRANCH + 8 * LEAF
    leaf_devices = lax.axis_size("leaf")
    key_width = w_key.shape[1]
    key_heads = key_width // head_width
    view_start = (col_index * row_devices + row_index) * row_count
    tree_start = view_start // tree_length * tree_length
    sub = math.gcd(row_count, KEY_BLOCK)
    own_place = lax.dynamic_slice_in_dim(
        position,
        ((leaf_index * row_devices + row_index) * col_devices + col_index) * row_count,
        row_count,
    )
    plan = key_plan(
        parents,
        segment,
        position,
        row_count,
        view_start,
        tree_start,
        tree_length,
        sub,
        leaf_index,
        (leaf_devices, row_devices, col_devices),
    )
    spread = leaf_devices * col_devices
    spot = leaf_index * col_devices + col_index
    stream_in = hidden_in.astype(jnp.float32)
    normed, in_back = jax.vjp(rms_norm, stream_in, norm_in)
    normed_b = normed.astype(bf16)
    own_cos, own_sin = rope_tables(own_place)

    def prep_fn(raw, gain):
        return head_prep(raw, gain, own_cos, own_sin)

    key_raw = product(normed_b, w_key)
    value_raw = product(normed_b, w_value)
    key_prep, key_back = jax.vjp(prep_fn, key_raw, key_norm)
    kv_own = jnp.concatenate([key_prep.reshape(row_count, key_width), value_raw], axis=1).astype(bf16)
    kv_block = lax.all_gather(kv_own, "row", axis=0, tiled=True)
    kv_tree = lax.all_gather(kv_block, "col", axis=0, tiled=True)
    if group_rows != tree_length:
        kv_tree = lax.dynamic_slice_in_dim(kv_tree, tree_start, tree_length, 0)
    query_part = w_query.shape[0] // spread
    w_query_piece = lax.dynamic_slice_in_dim(w_query, spot * query_part, query_part, 0)
    w_query_piece = lax.all_gather(w_query_piece, "row", axis=1, tiled=True)
    w_query_all = lax.all_gather(w_query_piece, ("leaf", "col"), axis=0, tiled=True)
    out_part = w_out.shape[0] // spread
    w_out_piece = lax.dynamic_slice_in_dim(w_out, spot * out_part, out_part, 0)
    w_out_piece = lax.all_gather(w_out_piece, "row", axis=0)
    w_out_all = lax.all_gather(w_out_piece, ("leaf", "col"), axis=1)
    w_out_all = w_out_all.reshape(w_query_all.shape[1], w_out.shape[1])
    query_raw = product(normed_b, w_query_all)
    query_prep, query_back = jax.vjp(prep_fn, query_raw, query_norm)
    query_b = query_prep.astype(bf16).reshape(row_count, -1)
    attended_b, lse = attend(plan, query_b, kv_tree, sub)
    attn_raw = product(attended_b, w_out_all)
    laurel_mid_b = product(normed_b, laurel_left).astype(bf16)
    laurel_raw = product(laurel_mid_b, laurel_right)

    def mix_one(stream_zero, attn_part, normed_part, laurel_part, attn_gain, laurel_gain):
        return (
            stream_zero
            + rms_norm(attn_part, attn_gain)
            + normed_part
            + rms_norm(laurel_part, laurel_gain)
        ) * INV_ROOT2

    stream_one, mix_back = jax.vjp(
        mix_one, stream_in, attn_raw, normed, laurel_raw, post_attn_norm, laurel_norm
    )
    ffn_input, ffn_in_back = jax.vjp(rms_norm, stream_one, pre_ffn_norm)
    ffn_input_b = ffn_input.astype(bf16)
    ffn_gathered = lax.all_gather(ffn_input_b, "row", axis=0, tiled=True)
    gate_value = product(ffn_gathered, w_gate)
    up_value = product(ffn_gathered, w_up)
    gelu_gate, gelu_back = jax.vjp(gelu_tanh, gate_value)
    hidden_b = (gelu_gate * up_value).astype(bf16)
    ffn_raw = lax.psum_scatter(
        product(hidden_b, w_down).astype(bf16), "row", scatter_dimension=0, tiled=True
    ).astype(jnp.float32)

    def mix_two(stream_part, ffn_part, ffn_gain):
        return stream_part + rms_norm(ffn_part, ffn_gain)

    stream_two, two_back = jax.vjp(mix_two, stream_one, ffn_raw, post_ffn_norm)
    stream_two_b = stream_two.astype(bf16)
    side_pre = product(stream_two_b, per_layer_gate)
    side_input = per_layer_in.astype(jnp.float32)
    side_act, side_act_back = jax.vjp(gelu_tanh, side_pre)
    side_b = (side_act * side_input).astype(bf16)
    side_raw = product(side_b, per_layer_proj)

    def mix_three(stream_part, side_part, side_gain):
        return stream_part + rms_norm(side_part, side_gain)

    output, three_back = jax.vjp(mix_three, stream_two, side_raw, per_layer_norm)
    grad_out = cotangent.astype(jnp.float32)
    grad_two, grad_side_raw, per_layer_norm_grad = three_back(grad_out)
    grad_side_b = grad_side_raw.astype(bf16)
    per_layer_proj_grad = product_tn(side_b, grad_side_b)
    grad_side = product_nt(grad_side_b, per_layer_proj)
    per_layer_in_grad = grad_side * side_act
    grad_pre_b = side_act_back(grad_side * side_input)[0].astype(bf16)
    per_layer_gate_grad = product_tn(stream_two_b, grad_pre_b)
    grad_two = grad_two + product_nt(grad_pre_b, per_layer_gate)
    grad_one, grad_ffn_raw, post_ffn_norm_grad = two_back(grad_two)
    grad_ffn_b = grad_ffn_raw.astype(bf16)
    grad_ffn_rows = lax.all_gather(grad_ffn_b, "row", axis=0, tiled=True)
    grad_hidden = product_nt(grad_ffn_rows, w_down)
    w_down_grad = product_tn(hidden_b, grad_ffn_rows)
    grad_gate_b = gelu_back(grad_hidden * up_value)[0].astype(bf16)
    grad_up_b = (grad_hidden * gelu_gate).astype(bf16)
    w_gate_grad = product_tn(ffn_gathered, grad_gate_b)
    w_up_grad = product_tn(ffn_gathered, grad_up_b)
    grad_ffn_input = lax.psum_scatter(
        (product_nt(grad_gate_b, w_gate) + product_nt(grad_up_b, w_up)).astype(jnp.bfloat16),
        "row",
        scatter_dimension=0,
        tiled=True,
    ).astype(jnp.float32)
    grad_one_extra, pre_ffn_norm_grad = ffn_in_back(grad_ffn_input)
    grad_one = grad_one + grad_one_extra
    (
        grad_zero,
        grad_attn_raw,
        grad_normed,
        grad_laurel_raw,
        post_attn_norm_grad,
        laurel_norm_grad,
    ) = mix_back(grad_one)
    grad_laurel_b = grad_laurel_raw.astype(bf16)
    laurel_right_grad = product_tn(laurel_mid_b, grad_laurel_b)
    grad_mid_b = product_nt(grad_laurel_b, laurel_right).astype(bf16)
    laurel_left_grad = product_tn(normed_b, grad_mid_b)
    grad_normed = grad_normed + product_nt(grad_mid_b, laurel_left)
    grad_attn_b = grad_attn_raw.astype(bf16)
    grad_vec_b = product_nt(grad_attn_b, w_out_all).astype(bf16)
    w_out_grad = product_tn(attended_b, grad_attn_b).astype(bf16)
    middle = jnp.sum(
        (grad_vec_b.astype(jnp.float32) * attended_b.astype(jnp.float32)).reshape(
            row_count, H, head_width
        ),
        axis=2,
    )
    middle = middle.reshape(row_count // sub, sub, key_heads, H // key_heads)
    middle = jnp.transpose(middle, (0, 2, 3, 1)).reshape(row_count // sub, key_heads, 1, -1)
    grad_query, grad_kv = attend_back(plan, query_b, grad_vec_b, lse, middle, kv_tree, sub)
    grad_query_raw, query_norm_grad = query_back(
        grad_query.reshape(row_count, H, head_width)
    )
    grad_query_b = grad_query_raw.astype(bf16)
    w_query_grad = product_tn(normed_b, grad_query_b).astype(bf16)
    if group_rows != tree_length:
        grad_kv = lax.dynamic_update_slice(
            jnp.zeros((group_rows, 2 * key_width), bf16), grad_kv, (tree_start, 0)
        )
    grad_kv = lax.psum_scatter(grad_kv, "col", scatter_dimension=0, tiled=True)
    grad_kv = lax.psum_scatter(grad_kv, "row", scatter_dimension=0, tiled=True)
    grad_value_b = grad_kv[:, key_width:]
    grad_key_raw, key_norm_grad = key_back(
        grad_kv[:, :key_width].astype(jnp.float32).reshape(row_count, key_heads, head_width)
    )
    grad_key_b = grad_key_raw.astype(bf16)
    w_key_full = product_tn(normed_b, grad_key_b)
    w_value_full = product_tn(normed_b, grad_value_b)
    grad_normed = (
        grad_normed
        + product_nt(grad_query_b, w_query_all)
        + product_nt(grad_key_b, w_key)
        + product_nt(grad_value_b, w_value)
    )
    grad_in_norm, norm_in_grad = in_back(grad_normed)
    input_grad = grad_zero + grad_in_norm
    both = ("leaf", "col")
    down_shard = lax.psum_scatter(w_down_grad.astype(bf16), both, scatter_dimension=1, tiled=True)
    gate_shard = lax.psum_scatter(w_gate_grad.astype(bf16), both, scatter_dimension=0, tiled=True)
    up_shard = lax.psum_scatter(w_up_grad.astype(bf16), both, scatter_dimension=0, tiled=True)
    out_shard = lax.psum_scatter(w_out_grad, both, scatter_dimension=1, tiled=True)
    out_shard = lax.psum_scatter(out_shard, "row", scatter_dimension=0, tiled=True)
    query_shard = lax.psum_scatter(w_query_grad, both, scatter_dimension=0, tiled=True)
    query_shard = lax.psum_scatter(query_shard, "row", scatter_dimension=1, tiled=True)
    down_shard, gate_shard, up_shard, out_shard, query_shard = (
        shard.astype(jnp.float32)
        for shard in (down_shard, gate_shard, up_shard, out_shard, query_shard)
    )
    every = ("leaf", "row", "col")
    quarter = key_width // row_devices
    pair = jnp.stack(
        [part.reshape(-1, row_devices, quarter) for part in (w_key_full, w_value_full)], axis=2
    )
    pair = jnp.transpose(pair, (1, 0, 2, 3)).reshape(row_devices, -1, 2 * quarter).astype(bf16)
    pair = lax.psum_scatter(pair, "row", scatter_dimension=0, tiled=True)[0]
    pair = lax.psum(pair.astype(jnp.float32), both)
    key_grad_part = pair[:, :quarter]
    value_grad_part = pair[:, quarter:]
    early = lax.psum(
        (
            laurel_left_grad,
            laurel_right_grad,
            per_layer_gate_grad,
            per_layer_proj_grad,
        ),
        every,
    )
    late = lax.psum(
        (
            norm_in_grad,
            query_norm_grad,
            key_norm_grad,
            post_attn_norm_grad,
            laurel_norm_grad,
            pre_ffn_norm_grad,
            post_ffn_norm_grad,
            per_layer_norm_grad,
        ),
        every,
    )
    return (
        output,
        input_grad,
        per_layer_in_grad,
        late[0],
        query_shard,
        key_grad_part,
        value_grad_part,
        late[1],
        late[2],
        out_shard,
        late[3],
        early[0],
        early[1],
        late[4],
        late[5],
        gate_shard,
        up_shard,
        down_shard,
        late[6],
        early[2],
        early[3],
        late[7],
    )


def solution(mesh):
    in_specs = (
        P(("leaf", "row", "col"), None),
        P(("leaf", "row", "col"), None),
        P(("leaf", "row", "col"), None),
        P(),
        P(None, "row"),
        P(),
        P(),
        P(),
        P(),
        P("row", None),
        P(),
        P(),
        P(),
        P(),
        P(),
        P(None, "row"),
        P(None, "row"),
        P("row", None),
        P(),
        P(),
        P(),
        P(),
        P(),
        P(),
        P(),
    )
    out_specs = (
        P(("leaf", "row", "col"), None),
        P(("leaf", "row", "col"), None),
        P(("leaf", "row", "col"), None),
        P(),
        P(("leaf", "col"), "row"),
        P(None, "row"),
        P(None, "row"),
        P(),
        P(),
        P("row", ("leaf", "col")),
        P(),
        P(),
        P(),
        P(),
        P(),
        P(("leaf", "col"), "row"),
        P(("leaf", "col"), "row"),
        P("row", ("leaf", "col")),
        P(),
        P(),
        P(),
        P(),
    )
    return jax.shard_map(
        per_device, mesh=mesh, in_specs=in_specs, out_specs=out_specs, check_vma=False
    )
```

time: 2590 us -> 1860 us (0.72)
  waiting for transfers between devices: 1720 us -> 1340 us
  matrix products: 429 us -> 240 us
  local copies, waits for them, and re-layouts: 204 us -> 52.5 us
  other arithmetic: 168 us -> 74.2 us
  Pallas kernels: 0 us -> 87.8 us
    reduce_scatter x9 -> x11, waiting for transfers between devices: 1050 us -> 630 us  [the longest x1 104 us: per_device(): grad_kv = lax.psum_scatter(grad_kv, 'col', scatter_dimension=0, tiled=True)]
    pallas_call x0 -> x2, Pallas kernels: none -> 87.8 us  [the longest x1 53.5 us: attend_back(): pl.pallas_call(functools.partial(attend_back_kernel, width ** (-0.5), key...]
    dot_general x15 -> x11, matrix products: 167 us -> 87.5 us  [product_nt(): lax.dot_general(left, right, (((1,), (1,)), ((), ())), preferred_element_...]
    all_gather x4 -> x6, waiting for transfers between devices: 185 us -> 261 us  [the longest x1 94.1 us: per_device(): kv_tree = lax.all_gather(kv_block, 'col', axis=0, tiled=True)]
    gather x7 -> x0, local copies, waits for them, and re-layouts: 75.2 us -> none  [the longest x1 28.7 us: per_device(): key_place = position[key_ids]]
    dot_general x16 -> x11, matrix products: 135 us -> 73.5 us  [product(): return jnp.dot(left, right, preferred_element_type=jnp.float32)]
    dot_general x15 -> x11, matrix products: 127 us -> 78.7 us  [product_tn(): lax.dot_general(left, right, (((0,), (0,)), ((), ())), preferred_element_...]
    convert_element_type x8 -> x10, other arithmetic: 62 us -> 19.9 us  [the longest x5 11.9 us: per_device(): shard.astype(jnp.float32)]
  transfers between devices with their start and end apart: 17 -> 22, of which waited for: 15 -> 22; matrix products, arithmetic and copies ran while one was open for 13% -> 10% of each run, Pallas kernels for 0% -> 2%
where the time goes in v1:
time: 1860 us; the launch traced here: 1850 us
  waiting for transfers between devices  1340 us (72%)
  matrix products  240 us (13%)
  Pallas kernels  87.8 us (5%)
  other arithmetic  74.2 us (4%)
  local copies, waits for them, and re-layouts  52.5 us (3%)
  blocking collectives  40.4 us (2%)
    psum x1, waiting for transfers between devices, per_device(): lax.psum((laurel_left_grad, laurel_right_grad, per_layer_gate_grad, per_l...  149 us
    reduce_scatter x1, waiting for transfers between devices, per_device(): grad_kv = lax.psum_scatter(grad_kv, 'col', scatter_dimension=0, tiled=True)  104 us
    all_gather x1, waiting for transfers between devices, per_device(): grad_ffn_rows = lax.all_gather(grad_ffn_b, 'row', axis=0, tiled=True)  98.7 us
    all_gather x1, waiting for transfers between devices, per_device(): ffn_gathered = lax.all_gather(ffn_input_b, 'row', axis=0, tiled=True)  98 us
    all_gather x1, waiting for transfers between devices, per_device(): kv_tree = lax.all_gather(kv_block, 'col', axis=0, tiled=True)  94.1 us
    reduce_scatter x1, waiting for transfers between devices, per_device(): lax.psum_scatter(product(hidden_b, w_down).astype(bf16), 'row', scatter_d...  92.2 us
    reduce_scatter x1, waiting for transfers between devices, per_device(): lax.psum_scatter((product_nt(grad_gate_b, w_gate) + product_nt(grad_up_b,...  91.6 us
    dot_general x11, matrix products, product_nt(): lax.dot_general(left, right, (((1,), (1,)), ((), ())), preferred_element_...  87.5 us
  transfers between devices with their start and end apart: 22, of which 22 were waited for; matrix products, arithmetic and copies ran while one was open for 10% of the time, Pallas kernels for 2%

profile of v1, /device:TPU:0, one launch (start us, length us, event | category | flops | bytes accessed | tf_op | source)
XLA Modules:
  0.0 1851.5 jit_solution(571516374014218192)
XLA Ops:
  41.0 56.2 %all-gather.15.cloned.1.call-done = bf16[1280,1024]{1,0:T(8,128)(2,1)} async-done(((bf16[320,1024]{1,0:T(8,128)(2,1)}), bf16[1280,1024]{1,0:T(8,128)(2,1)}) %all-gather.15.cloned.1.call-update) | async-done | bytes 2621456 | tf_op jit(solution)/shard_map/all_gather | solution.py:359
  97.3 28.9 %all-gather.23.cloned.1.call-done = bf16[256,2048]{1,0:T(8,128)(2,1)} async-done(((bf16[64,2048]{1,0:T(8,128)(2,1)}), bf16[256,2048]{1,0:T(8,128)(2,1)}) %all-gather.23.cloned.1.call-update) | async-done | bytes 1048592 | tf_op jit(solution)/shard_map/all_gather | solution.py:369
  134.2 47.3 %all-gather.13.cloned.1.call-done = bf16[2048,2048]{1,0:T(8,128)(2,1)} async-done(((bf16[256,2048]{1,0:T(8,128)(2,1)}), bf16[2048,2048]{1,0:T(8,128)(2,1)}) %all-gather.13.cloned.1.call-update) | async-done | bytes 8388624 | tf_op jit(solution)/shard_map/all_gather | solution.py:366
  194.1 94.1 %all-gather.17.cloned.1.call-done.kv_ref = bf16[5120,1024]{1,0:T(8,128)(2,1)} async-done(((bf16[1280,1024]{1,0:T(8,128)(2,1)}), bf16[5120,1024]{1,0:T(8,128)(2,1)}) %all-gather.17.cloned.1.call-update) | async-done | bytes 10485776 | tf_op jit(solution)/shard_map/all_gather | solution.py:360
  288.2 34.2 %attend.1 = (bf16[320,2048]{1,0:T(8,128)(2,1)S(1)}, f32[5,2,8,256]{3,2,1,0:T(8,128)S(1)}) custom-call(s32[5,20]{1,0:T(8,128)S(1)} %select_reduce_fusion.idx, s32[5]{0:T(128)S(1)} %get-tuple-element.219.count, s32[5]{0:T(128)S(1)} %get-tuple-element.256.own, s32[5]{0:T(128)S(1)} %get-tuple-element.255.offset, bf16[320,2048]{1,0:T(8,128)(2,1)S(1)} %bitcast.101, ...), custom_call_target="tpu_custom_call" | custom-call | tf_op jit(solution)/shard_map/attend/pallas_call | solution.py:184
  324.2 20.1 %all-gather.25.cloned.1.call-done = bf16[4,512,2048]{2,1,0:T(8,128)(2,1)} async-done(((bf16[4,64,2048]{2,1,0:T(8,128)(2,1)}), bf16[4,512,2048]{2,1,0:T(8,128)(2,1)}) %all-gather.25.cloned.1.call-update) | async-done | bytes 8388624 | tf_op jit(solution)/shard_map/all_gather | solution.py:370
  355.4 98.0 %all-gather.19.cloned.1.call-done = bf16[1280,2048]{1,0:T(8,128)(2,1)} async-done(((bf16[320,2048]{1,0:T(8,128)(2,1)}), bf16[1280,2048]{1,0:T(8,128)(2,1)}) %all-gather.19.cloned.1.call-update) | async-done | bytes 5242896 | tf_op jit(solution)/shard_map/all_gather | solution.py:393
  470.8 21.6 %multiply_convert_fusion.1 = (bf16[1280,2048]{1,0:T(8,128)(2,1)}, f32[1280,2048]{1,0:T(8,128)}) fusion(f32[1280,2048]{1,0:T(8,128)} %fusion.84, bf16[1280,2048]{1,0:T(8,128)(2,1)} %all-gather.19.cloned.1.call-done, bf16[2048,2048]{1,0:T(8,128)(2,1)} %param.41), kind=kOutput, calls=%fused_computation.11 | convolution fusion | flops 10763632640 | bytes 39845888 | tf_op jit(solution)/shard_map/dot_general | solution.py:28
  507.1 92.2 %reduce-scatter.13.cloned.1.call-done = bf16[320,2048]{1,0:T(8,128)(2,1)} async-done(((bf16[1280,2048]{1,0:T(8,128)(2,1)}), bf16[320,2048]{1,0:T(8,128)(2,1)}) %reduce-scatter.13.cloned.1.call-update) | async-done | bytes 1310736 | tf_op jit(solution)/shard_map/reduce_scatter | solution.py:398
  618.0 98.7 %all-gather.21.cloned.1.call-done = bf16[1280,2048]{1,0:T(8,128)(2,1)} async-done(((bf16[320,2048]{1,0:T(8,128)(2,1)}), bf16[1280,2048]{1,0:T(8,128)(2,1)}) %all-gather.21.cloned.1.call-update) | async-done | bytes 5242896 | tf_op jit(solution)/shard_map/all_gather | solution.py:428
  716.7 29.1 %multiply_convert_fusion = (bf16[1280,2048]{1,0:T(8,128)(2,1)}, bf16[1280,2048]{1,0:T(8,128)(2,1)}) fusion(f32[1280,2048]{1,0:T(8,128)} %fusion.84, f32[1280,2048]{1,0:T(8,128)} %get-tuple-element.248, bf16[1280,2048]{1,0:T(8,128)(2,1)} %all-gather.21.cloned.1.call-done, bf16[2048,2048]{1,0:T(8,128)(2,1)} %param.42), kind=kOutput, calls=%fused_computation.10 | convolution fusion | flops 10800332800 | bytes 45088768 | tf_op jit(solution)/shard_map/dot_general | solution.py:32
  778.4 91.6 %reduce-scatter.15.cloned.1.call-done = bf16[320,2048]{1,0:T(8,128)(2,1)} async-done(((bf16[1280,2048]{1,0:T(8,128)(2,1)}), bf16[320,2048]{1,0:T(8,128)(2,1)}) %reduce-scatter.15.cloned.1.call-update) | async-done | bytes 1310736 | tf_op jit(solution)/shard_map/reduce_scatter | solution.py:435
  895.7 53.5 %attend_back.1 = (f32[320,2048]{1,0:T(8,128)}, bf16[5120,1024]{1,0:T(8,128)(2,1)}) custom-call(s32[5,20]{1,0:T(8,128)} %copy-done.3, s32[5]{0:T(128)} %copy-done.5, s32[5]{0:T(128)} %copy-done.4, s32[5]{0:T(128)} %copy-done.6, bf16[320,2048]{1,0:T(8,128)(2,1)} %bitcast.102, bf16[320,2048]{1,0:T(8,128)(2,1)} %get-tuple-element.253.d_ref, ...), custom_call_target="tpu_custom_call" | custom-call | tf_op jit(solution)/shard_map/attend_back/pallas_call | solution.py:217
  949.4 103.5 %reduce-scatter.17.cloned.1.call-done = bf16[1280,1024]{1,0:T(8,128)(2,1)} async-done(((bf16[5120,1024]{1,0:T(8,128)(2,1)}), bf16[1280,1024]{1,0:T(8,128)(2,1)}) %reduce-scatter.17.cloned.1.call-update) | async-done | bytes 2621456 | tf_op jit(solution)/shard_map/reduce_scatter | solution.py:477
  1082.5 24.9 %reduce-scatter.19.cloned.1.call-done = bf16[320,1024]{1,0:T(8,128)(2,1)} async-done(((bf16[1280,1024]{1,0:T(8,128)(2,1)}), bf16[320,1024]{1,0:T(8,128)(2,1)}) %reduce-scatter.19.cloned.1.call-update) | async-done | bytes 655376 | tf_op jit(solution)/shard_map/reduce_scatter | solution.py:478
  1182.0 74.5 %reduce-scatter.27.cloned.1.call-done = bf16[2048,256]{1,0:T(8,128)(2,1)} async-done(((bf16[2048,2048]{1,0:T(8,128)(2,1)}), bf16[2048,256]{1,0:T(8,128)(2,1)}) %reduce-scatter.27.cloned.1.call-update) | async-done | bytes 1048592 | tf_op jit(solution)/shard_map/reduce_scatter | solution.py:498
  1260.2 75.2 %reduce-scatter.25.cloned.1.call-done = bf16[1,2048,256]{1,2,0:T(8,128)(2,1)} async-done(((bf16[4,2048,256]{1,2,0:T(8,128)(2,1)}), bf16[1,2048,256]{1,2,0:T(8,128)(2,1)}) %reduce-scatter.25.cloned.1.call-update) | async-done | bytes 1048592 | tf_op jit(solution)/shard_map/reduce_scatter | solution.py:512
  1354.2 56.6 %reduce-scatter.31.cloned.1.call-done = bf16[256,2048]{1,0:T(8,128)(2,1)} async-done(((bf16[2048,2048]{1,0:T(8,128)(2,1)}), bf16[256,2048]{1,0:T(8,128)(2,1)}) %reduce-scatter.31.cloned.1.call-update) | async-done | bytes 1048592 | tf_op jit(solution)/shard_map/reduce_scatter | solution.py:496
  1413.6 72.0 %reduce-scatter.33.cloned.1.call-done = bf16[256,2048]{1,0:T(8,128)(2,1)} async-done(((bf16[2048,2048]{1,0:T(8,128)(2,1)}), bf16[256,2048]{1,0:T(8,128)(2,1)}) %reduce-scatter.33.cloned.1.call-update) | async-done | bytes 1048592 | tf_op jit(solution)/shard_map/reduce_scatter | solution.py:497
  1488.4 71.9 %reduce-scatter.35.cloned.1.call-done = bf16[2048,256]{1,0:T(8,128)(2,1)} async-done(((bf16[2048,2048]{1,0:T(8,128)(2,1)}), bf16[2048,256]{1,0:T(8,128)(2,1)}) %reduce-scatter.35.cloned.1.call-update) | async-done | bytes 1048592 | tf_op jit(solution)/shard_map/reduce_scatter | solution.py:495
  1563.0 26.9 %reduce-scatter.23.cloned.1.call-done = bf16[256,512]{1,0:T(8,128)(2,1)} async-done(((bf16[256,2048]{1,0:T(8,128)(2,1)}), bf16[256,512]{1,0:T(8,128)(2,1)}) %reduce-scatter.23.cloned.1.call-update) | async-done | bytes 262160 | tf_op jit(solution)/shard_map/reduce_scatter | solution.py:501
  1591.7 26.1 %reduce-scatter.29.cloned.1.call-done = bf16[512,256]{1,0:T(8,128)(2,1)} async-done(((bf16[2048,256]{1,0:T(8,128)(2,1)}), bf16[512,256]{1,0:T(8,128)(2,1)}) %reduce-scatter.29.cloned.1.call-update) | async-done | bytes 262160 | tf_op jit(solution)/shard_map/reduce_scatter | solution.py:499
  1625.8 40.4 %all-reduce.4 = (f32[2048]{0:T(1024)}, f32[256]{0:T(256)}, f32[256]{0:T(256)}, f32[2048]{0:T(1024)}, f32[2048]{0:T(1024)}, /*index=5*/f32[2048]{0:T(1024)}, f32[2048]{0:T(1024)}, f32[2048]{0:T(1024)}) all-reduce(f32[2048]{0:T(1024)S(1)} %get-tuple-element.194, ...), channel_id=1, replica_groups=mesh['leaf'=2,'row'=4,'col'=4] {'leaf','row','col'}, use_global_device_ids=true, to_apply=%region_29.30 | all-reduce | flops 12800 | bytes 102400 | tf_op jit(solution)/shard_map/psum | solution.py:525
  1689.1 148.7 %all-reduce.11.cloned.1.call-done = (f32[2048,64]{0,1:T(8,128)}, f32[64,2048]{1,0:T(8,128)}, f32[2048,256]{1,0:T(8,128)}, f32[256,2048]{1,0:T(8,128)}) async-done(((f32[2048,64]{0,1:T(8,128)}, f32[64,2048]{1,0:T(8,128)}, f32[2048,256]{1,0:T(8,128)}, f32[256,2048]{1,0:T(8,128)}), (f32[2048,64]{0,1:T(8,128)}, f32[64,2048]{1,0:T(8,128)}, f32[2048,256]{1,0:T(8,128)}, ...) | async-done | bytes 5242896 | tf_op jit(solution)/shard_map/psum | solution.py:516
  (391 shorter events, 349.1 us)
Async XLA Ops:
  7.2 33.7 %all-gather.11.cloned.1.call-start = ((), (), s32[]{:S(2)}) async-start(), calls=%async_computation.12 | async-start | bytes 1310720 | tf_op jit(solution)/shard_map/all_gather | solution.py:365
  9.1 88.1 %all-gather.15.cloned.1.call-start = ((), (), s32[]{:S(2)}) async-start(), calls=%async_computation.14 | async-start | bytes 3276800 | tf_op jit(solution)/shard_map/all_gather | solution.py:359
  24.8 101.3 %all-gather.23.cloned.1.call-start = ((), (), s32[]{:S(2)}) async-start(), calls=%async_computation.31 | async-start | bytes 1310720 | tf_op jit(solution)/shard_map/all_gather | solution.py:369
  26.6 155.0 %all-gather.13.cloned.1.call-start = ((), (), s32[]{:S(2)}) async-start(), calls=%async_computation.13 | async-start | bytes 9437184 | tf_op jit(solution)/shard_map/all_gather | solution.py:366
  40.9 247.3 %all-gather.17.cloned.1.call-start = ((), (), s32[]{:S(2)}) async-start(), calls=%async_computation.15 | async-start | bytes 13107200 | tf_op jit(solution)/shard_map/all_gather | solution.py:360
  97.2 247.1 %all-gather.25.cloned.1.call-start = ((), (), s32[]{:S(2)}) async-start(), calls=%async_computation.32 | async-start | bytes 9437184 | tf_op jit(solution)/shard_map/all_gather | solution.py:370
  126.1 327.3 %all-gather.19.cloned.1.call-start = ((), (), s32[]{:S(2)}) async-start(), calls=%async_computation.16 | async-start | bytes 6553600 | tf_op jit(solution)/shard_map/all_gather | solution.py:393
  128.0 160.3 %copy-start.4 = (s32[5]{0:T(128)}, s32[5]{0:T(128)S(1)}, u32[]{:S(2)}) copy-start(s32[5]{0:T(128)S(1)} %get-tuple-element.256.own) | copy-start | bytes 64
  134.2 216.7 %copy-start.70 = (f32[320]{0:T(512)}, f32[320]{0:T(512)S(1)}, u32[]{:S(2)}) copy-start(f32[320]{0:T(512)S(1)} %fusion.60) | copy-start | bytes 3844
  355.2 244.1 %reduce-scatter.13.cloned.1.call-start = ((), (), s32[]{:S(2)}) async-start(), calls=%async_computation.17 | async-start | bytes 6553600 | tf_op jit(solution)/shard_map/reduce_scatter | solution.py:398
  507.1 209.6 %all-gather.21.cloned.1.call-start = ((), (), s32[]{:S(2)}) async-start(), calls=%async_computation.18 | async-start | bytes 6553600 | tf_op jit(solution)/shard_map/all_gather | solution.py:428
  618.0 252.1 %reduce-scatter.15.cloned.1.call-start = ((), (), s32[]{:S(2)}) async-start(), calls=%async_computation.19 | async-start | bytes 6553600 | tf_op jit(solution)/shard_map/reduce_scatter | solution.py:435
  777.8 275.1 %reduce-scatter.17.cloned.1.call-start = ((), (), s32[]{:S(2)}) async-start(), calls=%async_computation.20 | async-start | bytes 13107200 | tf_op jit(solution)/shard_map/reduce_scatter | solution.py:477
  949.3 158.0 %reduce-scatter.19.cloned.1.call-start = ((), (), s32[]{:S(2)}) async-start(), calls=%async_computation.21 | async-start | bytes 3276800 | tf_op jit(solution)/shard_map/reduce_scatter | solution.py:478
  1052.9 129.0 %reduce-scatter.21.cloned.1.call-start = ((), (), s32[]{:S(2)}) async-start(), calls=%async_computation.22 | async-start | bytes 9437184 | tf_op jit(solution)/shard_map/reduce_scatter | solution.py:500
  1074.3 182.2 %reduce-scatter.27.cloned.1.call-start = ((), (), s32[]{:S(2)}) async-start(), calls=%async_computation.26 | async-start | bytes 9437184 | tf_op jit(solution)/shard_map/reduce_scatter | solution.py:498
  1082.4 253.0 %reduce-scatter.25.cloned.1.call-start = ((), (), s32[]{:S(2)}) async-start(), calls=%async_computation.24 | async-start | bytes 5242880 | tf_op jit(solution)/shard_map/reduce_scatter | solution.py:512
  1124.7 286.1 %reduce-scatter.31.cloned.1.call-start = ((), (), s32[]{:S(2)}) async-start(), calls=%async_computation.28 | async-start | bytes 9437184 | tf_op jit(solution)/shard_map/reduce_scatter | solution.py:496
  1142.1 343.6 %reduce-scatter.33.cloned.1.call-start = ((), (), s32[]{:S(2)}) async-start(), calls=%async_computation.29 | async-start | bytes 9437184 | tf_op jit(solution)/shard_map/reduce_scatter | solution.py:497
  1159.0 401.3 %reduce-scatter.35.cloned.1.call-start = ((), (), s32[]{:S(2)}) async-start(), calls=%async_computation.30 | async-start | bytes 9437184 | tf_op jit(solution)/shard_map/reduce_scatter | solution.py:495
  1176.1 413.8 %reduce-scatter.23.cloned.1.call-start = ((), (), s32[]{:S(2)}) async-start(), calls=%async_computation.23 | async-start | bytes 1310720 | tf_op jit(solution)/shard_map/reduce_scatter | solution.py:501
  1181.9 436.0 %reduce-scatter.29.cloned.1.call-start = ((), (), s32[]{:S(2)}) async-start(), calls=%async_computation.27 | async-start | bytes 1310720 | tf_op jit(solution)/shard_map/reduce_scatter | solution.py:499
  1256.5 426.0 %all-reduce.9.cloned.1.call-start = ((), (), s32[]{:S(2)}) async-start(), calls=%async_computation.25 | async-start | bytes 4194304 | tf_op jit(solution)/shard_map/psum | solution.py:513
  1338.3 499.4 %all-reduce.11.cloned.1.call-start = ((), (), s32[]{:S(2)}) async-start(), calls=%async_computation.33 | async-start | bytes 10485760 | tf_op jit(solution)/shard_map/psum | solution.py:516
  (101 other events, 1854.1 us)
Sparse Core Ops, SparseCore 0:
  10.2 30.6 all-gather.10
  43.0 54.1 all-gather.14
  99.3 26.7 all-gather.22
  127.9 53.6 all-gather.12
  183.3 104.9 all-gather.16
  290.0 54.2 all-gather.24
  355.3 98.0 all-gather.18
  507.2 92.0 reduce-scatter.12
  618.1 98.5 all-gather.20
  777.9 92.1 reduce-scatter.14
  949.4 103.3 reduce-scatter.16
  1055.0 52.2 reduce-scatter.18
  1110.8 71.0 reduce-scatter.20
  1185.2 71.2 reduce-scatter.26
  1258.6 76.7 reduce-scatter.24
  1338.8 71.9 reduce-scatter.30
  1414.1 71.4 reduce-scatter.32
  1489.0 71.2 reduce-scatter.34
  1562.6 27.2 reduce-scatter.22
  1592.0 25.7 reduce-scatter.28
  1621.7 60.8 all-reduce.8
  1689.8 147.9 all-reduce.10
